TPU v7x, 32 devices: a whole 2x2x4 slice. The times are simulated.
32 devices in a mesh: dp: 16 (over z, y, core), tensor: 2 (over x).
Axes of the slice: x: 2, y: 2, z: 4, core: 2. Of those that a mesh axis runs over, the one named last changes fastest.
Arguments:
- tokens: bfloat16 [8192, 640], P(('dp', 'tensor')), may hold values from -40 to 40
- segment_ids: int32 [8192], P('dp'), may hold values from 0 to 8, as said below
- query_weight: bfloat16 [640, 1024], P('dp', 'tensor'), may hold values from -1 to 1
- key_weight: bfloat16 [640, 256], P('dp'), may hold values from -1 to 1
- value_weight: bfloat16 [640, 256], P('dp'), may hold values from -0.25 to 0.25
- out_weight: bfloat16 [1024, 640], P('tensor', 'dp'), may hold values from -1 to 1
- gate_weight: bfloat16 [640, 2048], P('dp', 'tensor'), may hold values from -0.25 to 0.25
- up_weight: bfloat16 [640, 2048], P('dp', 'tensor'), may hold values from -0.25 to 0.25
- down_weight: bfloat16 [2048, 640], P('tensor', 'dp'), may hold values from -1 to 1
- gain_before_attention: bfloat16 [640], P('dp'), may hold values from 0.25 to 1.75
- gain_after_attention: bfloat16 [640], P('dp'), may hold values from 0.25 to 1.75
- gain_before_feed: bfloat16 [640], P('dp'), may hold values from 0.25 to 1.75
- gain_after_feed: bfloat16 [640], P('dp'), may hold values from 0.25 to 1.75
- query_gain: bfloat16 [256], P('dp'), may hold values from 0.25 to 1.75
- key_gain: bfloat16 [256], P('dp'), may hold values from 0.25 to 1.75
- cotangent: float32 [8192, 640], P(('dp', 'tensor')), may hold values from -6 to 6
Outputs:
- outputs: float32 [8192, 640], P(('dp', 'tensor'))
- tokens_grad: float32 [8192, 640], P(('dp', 'tensor'))
- query_weight_grad: float32 [640, 1024], P('dp', 'tensor')
- key_weight_grad: float32 [640, 256], P('dp')
- value_weight_grad: float32 [640, 256], P('dp')
- out_weight_grad: float32 [1024, 640], P('tensor', 'dp')
- gate_weight_grad: float32 [640, 2048], P('dp', 'tensor')
- up_weight_grad: float32 [640, 2048], P('dp', 'tensor')
- down_weight_grad: float32 [2048, 640], P('tensor', 'dp')
- gain_before_attention_grad: float32 [640], P('dp')
- gain_after_attention_grad: float32 [640], P('dp')
- gain_before_feed_grad: float32 [640], P('dp')
- gain_after_feed_grad: float32 [640], P('dp')
- query_gain_grad: float32 [256], P('dp')
- key_gain_grad: float32 [256], P('dp')
Inputs may be any that keep to these rules, and one draw needn't show every extreme that they name: `segment_ids`: within each aligned block of 512 tokens the numbers never fall; a document is a run of equal numbers inside one such block; in some block one document fills all 512 tokens.
All inputs are finite; a program needn't handle non-finite values.
Results may differ from a plain program's by a relative error of at most 0.019.
Values may be sent and summed in bfloat16 or wider, within the bound.
A program may use at most 128 MiB of HBM per device.

v0:
```python
import math

import jax
import jax.numpy as jnp
from jax import lax
from jax.sharding import PartitionSpec as P

HD = 256
WINDOW = 512


EPS = 1e-06
ROPE_BASE = 10000.0


def norm_fwd(values, gain):
    inverse = lax.rsqrt(jnp.mean(values * values, axis=-1, keepdims=True) + EPS)
    return values * inverse * gain


def norm_back(values, gain, grad_out):
    inverse = lax.rsqrt(jnp.mean(values * values, axis=-1, keepdims=True) + EPS)
    unit_rows = values * inverse
    scaled = grad_out * gain
    grad_in = inverse * (scaled - unit_rows * jnp.mean(scaled * unit_rows, axis=-1, keepdims=True))
    grad_gain = jnp.sum((grad_out * unit_rows).reshape(-1, values.shape[-1]), axis=0)
    return (grad_in, grad_gain)


def gelu_parts(gate_pre):
    factor = math.sqrt(2.0 / math.pi)
    tangent = jnp.tanh(factor * (gate_pre + 0.044715 * gate_pre * gate_pre * gate_pre))
    value_out = 0.5 * gate_pre * (1.0 + tangent)
    slope = 0.5 * (1.0 + tangent) + 0.5 * gate_pre * (1.0 - tangent * tangent) * factor * (
        1.0 + 3.0 * 0.044715 * gate_pre * gate_pre
    )
    return (value_out, slope)


def rope_tables(segments):
    earlier = jnp.sum((segments[None, :] < segments[:, None]).astype(jnp.int32), axis=1)
    place = (jnp.arange(segments.shape[0], dtype=jnp.int32) - earlier).astype(jnp.float32)
    half_width = HD // 2
    freq = jnp.exp(-(2.0 * jnp.arange(half_width, dtype=jnp.float32) / HD) * math.log(ROPE_BASE))
    angle = place[:, None] * freq[None, :]
    return (jnp.cos(angle), jnp.sin(angle))


def rotate(vals, cosine, sine_table):
    half_width = vals.shape[-1] // 2
    first_half = vals[..., :half_width]
    second = vals[..., half_width:]
    return jnp.concatenate(
        [first_half * cosine - second * sine_table, second * cosine + first_half * sine_table],
        axis=-1,
    )


def unrotate(grads, cosine, sine_table):
    half_width = grads.shape[-1] // 2
    first_half = grads[..., :half_width]
    second = grads[..., half_width:]
    return jnp.concatenate(
        [first_half * cosine + second * sine_table, second * cosine - first_half * sine_table],
        axis=-1,
    )


def allowed_pairs(seg_query, seg_key, query_first, key_first):
    query_pos = query_first + jnp.arange(seg_query.shape[0], dtype=jnp.int32)
    key_pos = key_first + jnp.arange(seg_key.shape[0], dtype=jnp.int32)
    spacing = query_pos[:, None] - key_pos[None, :]
    return (seg_query[:, None] == seg_key[None, :]) & (spacing >= 0) & (spacing < WINDOW)


def block_spans(total_rows):
    block_rows = min(512, total_rows)
    key_first = max(0 - block_rows, 0)
    spans = [(0, block_rows, key_first, block_rows)]
    return spans


def spread_rows(piece):
    return lax.all_gather(piece, "tensor", axis=0, tiled=True)


def spread_grads(piece):
    return lax.all_gather(piece, "tensor", axis=0, tiled=True)


def collect_rows(left, right, own_rows):

    def term(row_start, row_count):
        return jnp.dot(left, right, preferred_element_type=jnp.float32)

    return lax.psum_scatter(
        term(jnp.int32(0), own_rows * lax.axis_size("tensor")),
        "tensor",
        scatter_dimension=0,
        tiled=True,
    )


def collect_grads(lefts, rights, own_rows):

    def term(row_start, row_count):
        summed = jnp.zeros((row_count, rights[0].shape[0]), jnp.float32)
        for left_part, right_part in zip(lefts, rights):
            summed = summed + jnp.dot(left_part, right_part.T, preferred_element_type=jnp.float32)
        return summed

    return lax.psum_scatter(
        term(jnp.int32(0), own_rows * lax.axis_size("tensor")).astype(jnp.bfloat16),
        "tensor",
        scatter_dimension=0,
        tiled=True,
    ).astype(jnp.float32)


def body(
    tokens,
    segment_ids,
    query_weight,
    key_weight,
    value_weight,
    out_weight,
    gate_weight,
    up_weight,
    down_weight,
    gain_before_attention,
    gain_after_attention,
    gain_before_feed,
    gain_after_feed,
    query_gain,
    key_gain,
    cotangent,
):
    f32 = jnp.float32
    bf16 = jnp.bfloat16
    own_rows = tokens.shape[0]
    total_rows = own_rows * lax.axis_size("tensor")
    own_start = lax.axis_index("tensor") * own_rows
    scale = HD ** (-0.5)
    attention_full = (
        lax.all_gather(query_weight, "dp", axis=0, tiled=True),
        lax.all_gather(key_weight, "dp", axis=0, tiled=True),
        lax.all_gather(value_weight, "dp", axis=0, tiled=True),
        lax.all_gather(out_weight, "dp", axis=1, tiled=True),
        lax.all_gather(gain_before_attention, "dp", axis=0, tiled=True),
        lax.all_gather(gain_after_attention, "dp", axis=0, tiled=True),
        lax.all_gather(query_gain, "dp", axis=0, tiled=True),
        lax.all_gather(key_gain, "dp", axis=0, tiled=True),
    )
    query_full, key_full, value_full, out_full = (
        attention_full[0],
        attention_full[1],
        attention_full[2],
        attention_full[3],
    )
    gain_ai = attention_full[4].astype(f32)
    gain_ao = attention_full[5].astype(f32)
    gain_query = attention_full[6].astype(f32)
    gain_key = attention_full[7].astype(f32)
    feed_full = (
        lax.all_gather(gate_weight, "dp", axis=0, tiled=True),
        lax.all_gather(up_weight, "dp", axis=0, tiled=True),
        lax.all_gather(down_weight, "dp", axis=1, tiled=True),
        lax.all_gather(gain_before_feed, "dp", axis=0, tiled=True),
        lax.all_gather(gain_after_feed, "dp", axis=0, tiled=True),
    )
    gate_full, up_full, down_full = (feed_full[0], feed_full[1], feed_full[2])
    gain_fi = feed_full[3].astype(f32)
    gain_fo = feed_full[4].astype(f32)
    local_heads = query_full.shape[1] // HD
    x_rows = tokens.astype(f32)
    normed_own = norm_fwd(x_rows, gain_ai).astype(bf16)
    normed_in = spread_rows(normed_own)
    queries = jnp.dot(normed_in, query_full, preferred_element_type=f32).reshape(
        total_rows, local_heads, HD
    )
    key_rows = jnp.dot(normed_in, key_full, preferred_element_type=f32)
    value_rows = jnp.dot(normed_in, value_full, preferred_element_type=f32).astype(bf16)
    cosine, sine_table = rope_tables(segment_ids)
    query_rot = (
        rotate(norm_fwd(queries, gain_query), cosine[:, None, :], sine_table[:, None, :]) * scale
    ).astype(bf16)
    key_rot = rotate(norm_fwd(key_rows, gain_key), cosine, sine_table).astype(bf16)
    spans = block_spans(total_rows)
    attended_parts = []
    log_parts = []
    for query_first, block_rows, key_first, key_end in spans:
        allowed = allowed_pairs(segment_ids, segment_ids, query_first, key_first)[None]
        scores = jnp.einsum("qhd,kd->hqk", query_rot, key_rot, preferred_element_type=f32)
        exp_total = jnp.sum(jnp.where(allowed, jnp.exp(scores), 0.0), axis=-1, keepdims=True)
        log_total = jnp.log(exp_total)
        probs_b = jnp.where(allowed, jnp.exp(scores - log_total), 0.0).astype(bf16)
        attended_parts.append(
            jnp.einsum("hqk,kd->qhd", probs_b, value_rows, preferred_element_type=f32)
        )
        log_parts.append(log_total)
    attended = attended_parts[0].reshape(total_rows, local_heads * HD).astype(bf16)
    mixed = collect_rows(attended, out_full, own_rows)
    hidden_state = x_rows + norm_fwd(mixed, gain_ao)
    normed_mid_own = norm_fwd(hidden_state, gain_fi).astype(bf16)
    normed_mid = spread_rows(normed_mid_own)
    gate_pre = jnp.dot(normed_mid, gate_full, preferred_element_type=f32)
    up_values = jnp.dot(normed_mid, up_full, preferred_element_type=f32)
    gelu_value, gelu_slope = gelu_parts(gate_pre)
    activated = (gelu_value * up_values).astype(bf16)
    feed_out = collect_rows(activated, down_full, own_rows)
    result = hidden_state + norm_fwd(feed_out, gain_fo)
    feed_back = (
        lax.all_gather(gate_weight, "dp", axis=0, tiled=True),
        lax.all_gather(up_weight, "dp", axis=0, tiled=True),
        lax.all_gather(down_weight, "dp", axis=1, tiled=True),
    )
    gate_back, up_back, down_back = (feed_back[0], feed_back[1], feed_back[2])
    attention_back = (
        lax.all_gather(query_weight, "dp", axis=0, tiled=True),
        lax.all_gather(key_weight, "dp", axis=0, tiled=True),
        lax.all_gather(value_weight, "dp", axis=0, tiled=True),
        lax.all_gather(out_weight, "dp", axis=1, tiled=True),
    )
    query_back, key_back, value_back, out_back = (
        attention_back[0],
        attention_back[1],
        attention_back[2],
        attention_back[3],
    )
    grad_feed, grad_gfo = norm_back(feed_out, gain_fo, cotangent)
    grad_feed_all = spread_grads(grad_feed.astype(bf16))
    grad_act = jnp.dot(grad_feed_all, down_back.T, preferred_element_type=f32)
    grad_down = jnp.dot(activated.T, grad_feed_all, preferred_element_type=f32)
    grad_gate_b = (grad_act * up_values * gelu_slope).astype(bf16)
    grad_up_b = (grad_act * gelu_value).astype(bf16)
    grad_gate_w = jnp.dot(normed_mid.T, grad_gate_b, preferred_element_type=f32)
    grad_up_w = jnp.dot(normed_mid.T, grad_up_b, preferred_element_type=f32)
    grad_mid = collect_grads((grad_gate_b, grad_up_b), (gate_back, up_back), own_rows)
    grad_mid_in, grad_gfi = norm_back(hidden_state, gain_fi, grad_mid)
    grad_hidden = cotangent + grad_mid_in
    feed_shards = (
        lax.psum_scatter(grad_gate_w, "dp", scatter_dimension=0, tiled=True),
        lax.psum_scatter(grad_up_w, "dp", scatter_dimension=0, tiled=True),
        lax.psum_scatter(grad_down, "dp", scatter_dimension=1, tiled=True),
        lax.psum_scatter(grad_gfi, "dp", scatter_dimension=0, tiled=True),
        lax.psum_scatter(grad_gfo, "dp", scatter_dimension=0, tiled=True),
    )
    grad_mixed, grad_gao = norm_back(mixed, gain_ao, grad_hidden)
    grad_mixed_all = spread_grads(grad_mixed.astype(bf16))
    grad_attended = jnp.dot(grad_mixed_all, out_back.T, preferred_element_type=f32).astype(bf16)
    grad_out_w = jnp.dot(attended.T, grad_mixed_all, preferred_element_type=f32)
    grad_heads = grad_attended.reshape(total_rows, local_heads, HD)
    grad_krot = jnp.zeros((total_rows, HD), f32)
    grad_vpart = jnp.zeros((total_rows, HD), f32)
    query_first, block_rows, key_first, key_end = spans[0]
    allowed = allowed_pairs(segment_ids, segment_ids, query_first, key_first)[None]
    scores = jnp.einsum("qhd,kd->hqk", query_rot, key_rot, preferred_element_type=f32)
    probs = jnp.where(allowed, jnp.exp(scores - log_parts[0]), 0.0)
    probs_b = probs.astype(bf16)
    grad_probs = jnp.einsum("qhd,kd->hqk", grad_heads, value_rows, preferred_element_type=f32)
    grad_scores = (
        probs * (grad_probs - jnp.sum(probs * grad_probs, axis=-1, keepdims=True))
    ).astype(bf16)
    grad_qparts = jnp.einsum("hqk,kd->qhd", grad_scores, key_rot, preferred_element_type=f32)
    grad_krot = grad_krot.at[key_first:key_end].add(
        jnp.einsum("hqk,qhd->kd", grad_scores, query_rot, preferred_element_type=f32)
    )
    grad_vpart = grad_vpart.at[key_first:key_end].add(
        jnp.einsum("hqk,qhd->kd", probs_b, grad_heads, preferred_element_type=f32)
    )
    grad_krot, grad_value = (
        lax.psum(grad_krot.astype(jnp.bfloat16), "tensor").astype(jnp.float32),
        lax.psum(grad_vpart.astype(jnp.bfloat16), "tensor").astype(jnp.float32),
    )
    grad_value_b = grad_value.astype(bf16)
    grad_qunit = unrotate(grad_qparts * scale, cosine[:, None, :], sine_table[:, None, :])
    grad_kunit = unrotate(grad_krot, cosine, sine_table)
    grad_queries, grad_gq = norm_back(queries, gain_query, grad_qunit)
    grad_keys, grad_gk = norm_back(key_rows, gain_key, grad_kunit)
    grad_queries_b = grad_queries.reshape(total_rows, local_heads * HD).astype(bf16)
    grad_keys_b = grad_keys.astype(bf16)
    grad_query_w = jnp.dot(normed_in.T, grad_queries_b, preferred_element_type=f32)
    grad_key_w = jnp.dot(normed_in.T, grad_keys_b, preferred_element_type=f32)
    grad_value_w = jnp.dot(normed_in.T, grad_value_b, preferred_element_type=f32)
    grad_normed = collect_grads((grad_queries_b,), (query_back,), own_rows)
    own_keys = lax.dynamic_slice_in_dim(grad_keys_b, own_start, own_rows, 0)
    own_values = lax.dynamic_slice_in_dim(grad_value_b, own_start, own_rows, 0)
    grad_normed = (
        grad_normed
        + jnp.dot(own_keys, key_back.T, preferred_element_type=f32)
        + jnp.dot(own_values, value_back.T, preferred_element_type=f32)
    )
    grad_in_rows, grad_gai = norm_back(x_rows, gain_ai, grad_normed)
    grad_tokens = grad_hidden + grad_in_rows
    attention_shards = (
        lax.psum_scatter(grad_query_w, "dp", scatter_dimension=0, tiled=True),
        lax.psum_scatter(grad_key_w, "dp", scatter_dimension=0, tiled=True),
        lax.psum_scatter(grad_value_w, "dp", scatter_dimension=0, tiled=True),
        lax.psum_scatter(grad_out_w, "dp", scatter_dimension=1, tiled=True),
        lax.psum_scatter(grad_gai, "dp", scatter_dimension=0, tiled=True),
        lax.psum_scatter(grad_gao, "dp", scatter_dimension=0, tiled=True),
        lax.psum_scatter(grad_gq, "dp", scatter_dimension=0, tiled=True),
        lax.psum_scatter(grad_gk, "dp", scatter_dimension=0, tiled=True),
    )
    gain_totals = lax.psum(
        (
            attention_shards[4],
            attention_shards[5],
            feed_shards[3],
            feed_shards[4],
            attention_shards[6],
        ),
        "tensor",
    )
    return (
        result,
        grad_tokens,
        attention_shards[0],
        attention_shards[1],
        attention_shards[2],
        attention_shards[3],
        feed_shards[0],
        feed_shards[1],
        feed_shards[2],
        gain_totals[0],
        gain_totals[1],
        gain_totals[2],
        gain_totals[3],
        gain_totals[4],
        attention_shards[7],
    )


def solution(mesh):
    in_specs = (
        P(("dp", "tensor"), None),
        P("dp"),
        P("dp", "tensor"),
        P("dp", None),
        P("dp", None),
        P("tensor", "dp"),
        P("dp", "tensor"),
        P("dp", "tensor"),
        P("tensor", "dp"),
        P("dp"),
        P("dp"),
        P("dp"),
        P("dp"),
        P("dp"),
        P("dp"),
        P(("dp", "tensor"), None),
    )
    out_specs = (
        P(("dp", "tensor"), None),
        P(("dp", "tensor"), None),
        P("dp", "tensor"),
        P("dp", None),
        P("dp", None),
        P("tensor", "dp"),
        P("dp", "tensor"),
        P("dp", "tensor"),
        P("tensor", "dp"),
        P("dp"),
        P("dp"),
        P("dp"),
        P("dp"),
        P("dp"),
        P("dp"),
    )
    return jax.shard_map(body, mesh=mesh, in_specs=in_specs, out_specs=out_specs, check_vma=False)
```

profile of v0, /device:TPU:0, one launch (start us, length us, event | category | flops | bytes accessed | tf_op | source)
XLA Modules:
  0.0 873.6 jit_solution(8065185427715442507)
XLA Ops:
  18.9 36.6 %all-reduce.14 = (bf16[640]{0:T(1024)(128)(2,1)S(1)}, bf16[256]{0:T(256)(128)(2,1)S(1)}, bf16[256]{0:T(256)(128)(2,1)S(1)}, bf16[640]{0:T(1024)(128)(2,1)}, bf16...) all-reduce(bf16[640]{0:T(1024)(128)(2,1)S(1)} %dynamic-update-slice.4, ...), channel_id=1, replica_groups=mesh['dp'=16,'tensor'=2] {'dp'}, use_global_device_ids=true, to_apply=%add | all-reduce | flops 3072 | bytes 12288
  57.8 7.7 all_gather.59
  65.5 18.0 %all_gather.60 = bf16[640,256]{1,0:T(8,128)(2,1)S(1)} all-gather(bf16[40,256]{1,0:T(8,128)(2,1)S(1)} %copy-done.48), channel_id=1, replica_groups=mesh['dp'=16,'tensor'=2] {'dp'}, dimensions={0}, use_global_device_ids=true | all-gather | bytes 348160 | tf_op jit(solution)/shard_map/all_gather | solution.py:147
  83.5 20.2 %all_gather.61 = bf16[640,256]{1,0:T(8,128)(2,1)S(1)} all-gather(bf16[40,256]{1,0:T(8,128)(2,1)S(1)} %copy-done.49), channel_id=1, replica_groups=mesh['dp'=16,'tensor'=2] {'dp'}, dimensions={0}, use_global_device_ids=true | all-gather | bytes 348160 | tf_op jit(solution)/shard_map/all_gather | solution.py:146
  105.3 19.2 %all_gather.63 = bf16[640,512]{1,0:T(8,128)(2,1)S(1)} all-gather(bf16[40,512]{1,0:T(8,128)(2,1)S(1)} %copy-done.47), channel_id=1, replica_groups=mesh['dp'=16,'tensor'=2] {'dp'}, dimensions={0}, use_global_device_ids=true | all-gather | bytes 696320 | tf_op jit(solution)/shard_map/all_gather | solution.py:145
  130.3 22.3 %all_gather.65 = bf16[512,640]{0,1:T(8,128)(2,1)} all-gather(bf16[512,40]{0,1:T(8,128)(2,1)} %param.29), channel_id=1, replica_groups=mesh['dp'=16,'tensor'=2] {'dp'}, dimensions={1}, use_global_device_ids=true | all-gather | bytes 696320 | tf_op jit(solution)/shard_map/all_gather | solution.py:148
  156.4 3.5 convolution_convert_fusion.2
  163.6 18.8 %reduce-scatter.12.cloned.1.call-done = f32[256,640]{1,0:T(8,128)} async-done(((f32[512,640]{1,0:T(8,128)}), f32[256,640]{1,0:T(8,128)}) %reduce-scatter.12.cloned.1.call-update) | async-done | bytes 655376 | tf_op jit(solution)/shard_map/reduce_scatter | solution.py:96
  185.2 10.0 %all_gather.68 = bf16[512,640]{1,0:T(8,128)(2,1)S(1)} all-gather(bf16[256,640]{1,0:T(8,128)(2,1)S(1)} %multiply_convert_fusion.4), channel_id=1, replica_groups=mesh['dp'=16,'tensor'=2] {'tensor'}, dimensions={0}, use_global_device_ids=true | all-gather | bytes 983040 | tf_op jit(solution)/shard_map/all_gather | solution.py:84
  195.1 5.2 all-gather.4.cloned.1.call-done
  200.3 3.6 fusion.96
  203.9 36.3 %all-gather.6.cloned.1.call-done = bf16[640,1024]{1,0:T(8,128)(2,1)} async-done(((bf16[40,1024]{1,0:T(8,128)(2,1)}), bf16[640,1024]{1,0:T(8,128)(2,1)}) %all-gather.6.cloned.1.call-update) | async-done | bytes 1310736 | tf_op jit(solution)/shard_map/all_gather | solution.py:166
  240.2 4.9 multiply_convert_fusion.1
  245.1 34.9 %all-gather.8.cloned.1.call-done = bf16[1024,640]{0,1:T(8,128)(2,1)} async-done(((bf16[1024,40]{0,1:T(8,128)(2,1)}), bf16[1024,640]{0,1:T(8,128)(2,1)}) %all-gather.8.cloned.1.call-update) | async-done | bytes 1310736 | tf_op jit(solution)/shard_map/all_gather | solution.py:167
  280.0 3.7 fusion.97
  283.8 22.2 %reduce-scatter.14.cloned.1.call-done = f32[256,640]{1,0:T(8,128)} async-done(((f32[512,640]{1,0:T(8,128)}), f32[256,640]{1,0:T(8,128)}) %reduce-scatter.14.cloned.1.call-update) | async-done | bytes 655376 | tf_op jit(solution)/shard_map/reduce_scatter | solution.py:96
  310.6 10.2 %all_gather.73 = bf16[512,640]{1,0:T(8,128)(2,1)S(1)} all-gather(bf16[256,640]{1,0:T(8,128)(2,1)S(1)} %get-tuple-element.95), channel_id=1, replica_groups=mesh['dp'=16,'tensor'=2] {'tensor'}, dimensions={0}, use_global_device_ids=true | all-gather | bytes 983040 | tf_op jit(solution)/shard_map/all_gather | solution.py:88
  320.8 3.9 multiply_convert_fusion
  329.4 15.6 %reduce-scatter.16.cloned.1.call-done = bf16[256,640]{1,0:T(8,128)(2,1)} async-done(((bf16[512,640]{1,0:T(8,128)(2,1)}), bf16[256,640]{1,0:T(8,128)(2,1)}) %reduce-scatter.16.cloned.1.call-update) | async-done | bytes 327696 | tf_op jit(solution)/shard_map/reduce_scatter | solution.py:112
  349.5 10.1 %all_gather.74 = bf16[512,640]{1,0:T(8,128)(2,1)S(1)} all-gather(bf16[256,640]{1,0:T(8,128)(2,1)S(1)} %multiply_convert_fusion.2), channel_id=1, replica_groups=mesh['dp'=16,'tensor'=2] {'tensor'}, dimensions={0}, use_global_device_ids=true | all-gather | bytes 983040 | tf_op jit(solution)/shard_map/all_gather | solution.py:88
  366.1 4.0 fusion.21
  379.3 22.1 %all-reduce.18.cloned.1.call-done = (bf16[512,256]{0,1:T(8,128)(2,1)}, bf16[512,256]{1,0:T(8,128)(2,1)}) async-done(((bf16[512,256]{0,1:T(8,128)(2,1)}, bf16[512,256]{1,0:T(8,128)(2,1)}), (bf16[512,256]{0,1:T(8,128)(2,1)}, bf16[512,256]{1,0:T(8,128)(2,1)})) %all-reduce.18.cloned.1.call-update) | async-done | bytes 524304 | tf_op jit(solution)/shard_map/psum | solution.py:272
  407.3 2.8 fusion.100
  412.1 3.6 fusion.104
  429.5 61.1 %all-reduce.12 = (f32[640]{0:T(1024)S(1)}, f32[640]{0:T(1024)S(1)}, f32[640]{0:T(1024)S(1)}, f32[640]{0:T(1024)S(1)}, f32[256]{0:T(256)S(1)}, /*index=5*/f32[256]{0:T(256)S(1)}) all-reduce(f32[640]{0:T(1024)S(1)} %get-tuple-element.63, f32[640]{0:T(1024)S(1)} %copy-done.54, ...), channel_id=13, replica_groups=mesh['dp'=16,'tensor'=2] {'dp'}, use_global_device_ids=true, to_apply=%region_29.30.clone | all-reduce | flops 3072 | bytes 24576
  491.5 5.4 all-reduce.13
  498.0 41.9 %reduce-scatter.24.cloned.1.call-done = f32[40,256]{1,0:T(8,128)} async-done(((f32[640,256]{1,0:T(8,128)}), f32[40,256]{1,0:T(8,128)}) %reduce-scatter.24.cloned.1.call-update) | async-done | bytes 40976 | tf_op jit(solution)/shard_map/reduce_scatter | solution.py:298
  539.9 61.8 %reduce-scatter.20.cloned.1.call-done = f32[40,512]{1,0:T(8,128)} async-done(((f32[640,512]{1,0:T(8,128)}), f32[40,512]{1,0:T(8,128)}) %reduce-scatter.20.cloned.1.call-update) | async-done | bytes 81936 | tf_op jit(solution)/shard_map/reduce_scatter | solution.py:296
  601.7 61.9 %reduce-scatter.26.cloned.1.call-done = f32[512,40]{0,1:T(8,128)} async-done(((f32[512,640]{0,1:T(8,128)}), f32[512,40]{0,1:T(8,128)}) %reduce-scatter.26.cloned.1.call-update) | async-done | bytes 81936 | tf_op jit(solution)/shard_map/reduce_scatter | solution.py:299
  663.6 67.4 %reduce-scatter.28.cloned.1.call-done = f32[40,1024]{1,0:T(8,128)} async-done(((f32[640,1024]{1,0:T(8,128)}), f32[40,1024]{1,0:T(8,128)}) %reduce-scatter.28.cloned.1.call-update) | async-done | bytes 163856 | tf_op jit(solution)/shard_map/reduce_scatter | solution.py:242
  731.0 67.6 %reduce-scatter.30.cloned.1.call-done = f32[40,1024]{1,0:T(8,128)} async-done(((f32[640,1024]{1,0:T(8,128)}), f32[40,1024]{1,0:T(8,128)}) %reduce-scatter.30.cloned.1.call-update) | async-done | bytes 163856 | tf_op jit(solution)/shard_map/reduce_scatter | solution.py:243
  798.5 67.5 %reduce-scatter.32.cloned.1.call-done = f32[1024,40]{0,1:T(8,128)} async-done(((f32[1024,640]{0,1:T(8,128)}), f32[1024,40]{0,1:T(8,128)}) %reduce-scatter.32.cloned.1.call-update) | async-done | bytes 163856 | tf_op jit(solution)/shard_map/reduce_scatter | solution.py:244
  (266 shorter events, 80.1 us)
Async XLA Ops:
  8.0 57.5 %copy-start.48 = (bf16[40,256]{1,0:T(8,128)(2,1)S(1)}, bf16[40,256]{1,0:T(8,128)(2,1)}, u32[]{:S(2)}) copy-start(bf16[40,256]{1,0:T(8,128)(2,1)} %param.28) | copy-start | bytes 61444
  8.0 75.5 %copy-start.49 = (bf16[40,256]{1,0:T(8,128)(2,1)S(1)}, bf16[40,256]{1,0:T(8,128)(2,1)}, u32[]{:S(2)}) copy-start(bf16[40,256]{1,0:T(8,128)(2,1)} %param.27) | copy-start | bytes 61444
  8.0 174.4 %reduce-scatter.12.cloned.1.call-start = ((), (), s32[]{:S(2)}) async-start(), calls=%async_computation.11 | async-start | bytes 1966080 | tf_op jit(solution)/shard_map/reduce_scatter | solution.py:96
  57.8 47.5 %copy-start.47 = (bf16[40,512]{1,0:T(8,128)(2,1)S(1)}, bf16[40,512]{1,0:T(8,128)(2,1)}, u32[]{:S(2)}) copy-start(bf16[40,512]{1,0:T(8,128)(2,1)} %param.26) | copy-start | bytes 122884
  83.5 21.8 %copy-start.18 = (bf16[640,256]{1,0:T(8,128)(2,1)}, bf16[640,256]{1,0:T(8,128)(2,1)S(1)}, u32[]{:S(2)}) copy-start(bf16[640,256]{1,0:T(8,128)(2,1)S(1)} %all_gather.60) | copy-start | bytes 983044
  105.2 21.1 %copy-start.3 = (f32[512,256]{0,1:T(8,128)}, f32[512,256]{0,1:T(8,128)S(1)}, u32[]{:S(2)}) copy-start(f32[512,256]{0,1:T(8,128)S(1)} %get-tuple-element.108) | copy-start | bytes 1572868
  105.3 21.1 %copy-start.57 = (f32[256]{0:T(256)}, f32[256]{0:T(256)S(1)}, u32[]{:S(2)}) copy-start(f32[256]{0:T(256)S(1)} %convert_element_type.111) | copy-start | bytes 3076
  125.7 27.7 %copy-start.1 = (f32[512,2,256]{2,0,1:T(8,128)}, f32[512,2,256]{2,0,1:T(8,128)S(1)}, u32[]{:S(2)}) copy-start(f32[512,2,256]{2,0,1:T(8,128)S(1)} %copy.62) | copy-start | bytes 3145732
  129.1 24.5 %copy-start.28 = (f32[512,128]{1,0:T(8,128)}, f32[512,128]{1,0:T(8,128)S(1)}, u32[]{:S(2)}) copy-start(f32[512,128]{1,0:T(8,128)S(1)} %copy.64) | copy-start | bytes 786436
  130.3 23.3 %copy-start.29 = (f32[512,128]{1,0:T(8,128)}, f32[512,128]{1,0:T(8,128)S(1)}, u32[]{:S(2)}) copy-start(f32[512,128]{1,0:T(8,128)S(1)} %copy.63) | copy-start | bytes 786436
  160.0 23.6 %copy-start.30 = (bf16[256,2,512]{2,0,1:T(8,128)(2,1)}, bf16[256,2,512]{2,0,1:T(8,128)(2,1)S(1)}, u32[]{:S(2)}) copy-start(bf16[256,2,512]{2,0,1:T(8,128)(2,1)S(1)} %convolution_convert_fusion.2) | copy-start | bytes 1572868
  160.0 23.6 %copy-start.6 = (bf16[256,640]{1,0:T(8,128)(2,1)S(1)}, bf16[256,640]{1,0:T(8,128)(2,1)}, u32[]{:S(2)}) copy-start(bf16[256,640]{1,0:T(8,128)(2,1)} %param.24) | copy-start | bytes 983044
  161.7 38.6 %all-gather.4.cloned.1.call-start = ((), (), s32[]{:S(2)}) async-start(), calls=%async_computation.12 | async-start | bytes 1392640 | tf_op jit(solution)/shard_map/all_gather | solution.py:165
  162.3 77.9 %all-gather.6.cloned.1.call-start = ((), (), s32[]{:S(2)}) async-start(), calls=%async_computation.13 | async-start | bytes 1392640 | tf_op jit(solution)/shard_map/all_gather | solution.py:166
  162.9 117.1 %all-gather.8.cloned.1.call-start = ((), (), s32[]{:S(2)}) async-start(), calls=%async_computation.14 | async-start | bytes 1392640 | tf_op jit(solution)/shard_map/all_gather | solution.py:167
  163.5 142.5 %reduce-scatter.14.cloned.1.call-start = ((), (), s32[]{:S(2)}) async-start(), calls=%async_computation.15 | async-start | bytes 1966080 | tf_op jit(solution)/shard_map/reduce_scatter | solution.py:96
  283.7 61.2 %reduce-scatter.16.cloned.1.call-start = ((), (), s32[]{:S(2)}) async-start(), calls=%async_computation.16 | async-start | bytes 983040 | tf_op jit(solution)/shard_map/reduce_scatter | solution.py:112
  309.5 11.3 %copy-start.67 = (f32[512,1024]{1,0:T(8,128)S(1)}, f32[512,1024]{1,0:T(8,128)}, u32[]{:S(2)}) copy-start(f32[512,1024]{1,0:T(8,128)} %fusion.96) | copy-start | bytes 6291460
  328.7 72.7 %all-reduce.18.cloned.1.call-start = ((), (), s32[]{:S(2)}) async-start(), calls=%async_computation.25 | async-start | bytes 1048576 | tf_op jit(solution)/shard_map/psum | solution.py:272
  346.9 12.7 %copy-start.25 = (bf16[512,640]{0,1:T(8,128)(2,1)S(1)}, bf16[512,640]{0,1:T(8,128)(2,1)}, u32[]{:S(2)}) copy-start(bf16[512,640]{0,1:T(8,128)(2,1)} %all_gather.65) | copy-start | bytes 1966084
  372.6 55.0 %reduce-scatter.18.cloned.1.call-start = ((), (), s32[]{:S(2)}) async-start(), calls=%async_computation.17 | async-start | bytes 983040 | tf_op jit(solution)/shard_map/reduce_scatter | solution.py:112
  377.7 24.7 %copy-start.60 = (f32[128]{0:T(128)S(1)}, f32[128]{0:T(128)}, u32[]{:S(2)}) copy-start(f32[128]{0:T(128)} %multiply_exponential_fusion) | copy-start | bytes 1540
  377.7 25.9 %copy-start.4 = (f32[512,256]{0,1:T(8,128)S(1)}, f32[512,256]{0,1:T(8,128)}, u32[]{:S(2)}) copy-start(f32[512,256]{0,1:T(8,128)} %copy-done.3) | copy-start | bytes 1572868
  377.7 25.9 %copy-start.58 = (f32[256]{0:T(256)S(1)}, f32[256]{0:T(256)}, u32[]{:S(2)}) copy-start(f32[256]{0:T(256)} %copy-done.57) | copy-start | bytes 3076
  379.2 118.8 %reduce-scatter.22.cloned.1.call-start = ((), (), s32[]{:S(2)}) async-start(), calls=%async_computation.19 | async-start | bytes 696320 | tf_op jit(solution)/shard_map/reduce_scatter | solution.py:297
  405.9 133.9 %reduce-scatter.24.cloned.1.call-start = ((), (), s32[]{:S(2)}) async-start(), calls=%async_computation.20 | async-start | bytes 696320 | tf_op jit(solution)/shard_map/reduce_scatter | solution.py:298
  407.3 194.4 %reduce-scatter.20.cloned.1.call-start = ((), (), s32[]{:S(2)}) async-start(), calls=%async_computation.18 | async-start | bytes 1392640 | tf_op jit(solution)/shard_map/reduce_scatter | solution.py:296
  410.2 253.4 %reduce-scatter.26.cloned.1.call-start = ((), (), s32[]{:S(2)}) async-start(), calls=%async_computation.21 | async-start | bytes 1392640 | tf_op jit(solution)/shard_map/reduce_scatter | solution.py:299
  412.1 318.9 %reduce-scatter.28.cloned.1.call-start = ((), (), s32[]{:S(2)}) async-start(), calls=%async_computation.22 | async-start | bytes 2785280 | tf_op jit(solution)/shard_map/reduce_scatter | solution.py:242
  415.8 382.8 %reduce-scatter.30.cloned.1.call-start = ((), (), s32[]{:S(2)}) async-start(), calls=%async_computation.23 | async-start | bytes 2785280 | tf_op jit(solution)/shard_map/reduce_scatter | solution.py:243
  419.4 446.5 %reduce-scatter.32.cloned.1.call-start = ((), (), s32[]{:S(2)}) async-start(), calls=%async_computation.24 | async-start | bytes 2785280 | tf_op jit(solution)/shard_map/reduce_scatter | solution.py:244
  427.6 69.4 %copy-start.11 = (f32[256,640]{1,0:T(8,128)S(1)}, f32[256,640]{1,0:T(8,128)}, u32[]{:S(2)}) copy-start(f32[256,640]{1,0:T(8,128)} %copy-done.10) | copy-start | bytes 1966084
  (51 other events, 139.2 us)
Sparse Core Ops, SparseCore 0:
  161.9 20.4 reduce-scatter.11
  283.8 22.1 reduce-scatter.13
  328.8 16.0 reduce-scatter.15
  372.7 28.6 all-reduce.17
  403.5 16.0 reduce-scatter.17
  423.6 56.5 reduce-scatter.21
  484.3 55.5 reduce-scatter.23
  544.1 57.5 reduce-scatter.19
  605.9 57.6 reduce-scatter.25
  667.8 63.1 reduce-scatter.27
  735.3 63.1 reduce-scatter.29
  802.7 63.2 reduce-scatter.31
Sparse Core Ops, SparseCore 1:
  164.5 35.8 all-gather.3
  202.5 37.6 all-gather.5
  242.3 37.6 all-gather.7
where the time goes:
time: 875 us; the launch traced here: 874 us
  waiting for transfers between devices  525 us (60%)
  blocking collectives  221 us (25%)
  matrix products  54.5 us (6%)
  other arithmetic  32.2 us (4%)
  local copies, waits for them, and re-layouts  20.8 us (2%)
  between operations  19.5 us (2%)
    unnamed x2, blocking collectives  97.6 us
    reduce_scatter x1, waiting for transfers between devices, body(): lax.psum_scatter(grad_up_w, 'dp', scatter_dimension=0, tiled=True)  67.6 us
    reduce_scatter x1, waiting for transfers between devices, body(): lax.psum_scatter(grad_down, 'dp', scatter_dimension=1, tiled=True)  67.5 us
    reduce_scatter x1, waiting for transfers between devices, body(): lax.psum_scatter(grad_gate_w, 'dp', scatter_dimension=0, tiled=True)  67.4 us
    reduce_scatter x1, waiting for transfers between devices, body(): lax.psum_scatter(grad_out_w, 'dp', scatter_dimension=1, tiled=True)  61.9 us
    reduce_scatter x1, waiting for transfers between devices, body(): lax.psum_scatter(grad_query_w, 'dp', scatter_dimension=0, tiled=True)  61.8 us
    reduce_scatter x1, waiting for transfers between devices, body(): lax.psum_scatter(grad_value_w, 'dp', scatter_dimension=0, tiled=True)  41.9 us
    reduce_scatter x2, waiting for transfers between devices, collect_rows(): lax.psum_scatter(term(jnp.int32(0), own_rows * lax.axis_size('tensor')),...  41 us
  transfers between devices with their start and end apart: 15, of which 13 were waited for; matrix products, arithmetic and copies ran while one was open for 5% of the time, Pallas kernels for 0%

commit v1 on v0

v1 whole, which is shorter than its diff:
```python
import math

import jax
import jax.numpy as jnp
from jax import lax
from jax.experimental import pallas as pl
from jax.experimental.pallas import tpu as pltpu
from jax.sharding import PartitionSpec as P

HD = 256
WINDOW = 512


EPS = 1e-06
ROPE_BASE = 10000.0


def norm_fwd(values, gain):
    inverse = lax.rsqrt(jnp.mean(values * values, axis=-1, keepdims=True) + EPS)
    return values * inverse * gain


def norm_back(values, gain, grad_out):
    inverse = lax.rsqrt(jnp.mean(values * values, axis=-1, keepdims=True) + EPS)
    unit_rows = values * inverse
    scaled = grad_out * gain
    grad_in = inverse * (scaled - unit_rows * jnp.mean(scaled * unit_rows, axis=-1, keepdims=True))
    grad_gain = jnp.sum((grad_out * unit_rows).reshape(-1, values.shape[-1]), axis=0)
    return (grad_in, grad_gain)


def gelu_parts(gate_pre):
    factor = math.sqrt(2.0 / math.pi)
    tangent = jnp.tanh(factor * (gate_pre + 0.044715 * gate_pre * gate_pre * gate_pre))
    value_out = 0.5 * gate_pre * (1.0 + tangent)
    slope = 0.5 * (1.0 + tangent) + 0.5 * gate_pre * (1.0 - tangent * tangent) * factor * (
        1.0 + 3.0 * 0.044715 * gate_pre * gate_pre
    )
    return (value_out, slope)


def rope_tables(segments, position):
    earlier = jnp.sum((segments[None, :] < segments[:, None]).astype(jnp.int32), axis=1)
    place = (position - earlier).astype(jnp.float32)
    half_width = HD // 2
    freq = jnp.exp(-(2.0 * jnp.arange(half_width, dtype=jnp.float32) / HD) * math.log(ROPE_BASE))
    angle = place[:, None] * freq[None, :]
    return (jnp.cos(angle), jnp.sin(angle))


def rotate(vals, cosine, sine_table):
    half_width = vals.shape[-1] // 2
    first_half = vals[..., :half_width]
    second = vals[..., half_width:]
    return jnp.concatenate(
        [first_half * cosine - second * sine_table, second * cosine + first_half * sine_table],
        axis=-1,
    )


def unrotate(grads, cosine, sine_table):
    half_width = grads.shape[-1] // 2
    first_half = grads[..., :half_width]
    second = grads[..., half_width:]
    return jnp.concatenate(
        [first_half * cosine + second * sine_table, second * cosine - first_half * sine_table],
        axis=-1,
    )


def greet(partners):
    barrier = pltpu.get_barrier_semaphore()
    for axis, index in partners:
        pl.semaphore_signal(
            barrier, inc=1, device_id={axis: index}, device_id_type=pl.DeviceIdType.MESH
        )
    pl.semaphore_wait(barrier, len(partners))


def dp_place(size):
    me = lax.axis_index("dp")
    core = lax.rem(me, 2)
    side = lax.rem(me // 2, 2)
    depth = me // 4
    return me, depth, side, core


def dp_index(depth, side, core):
    return depth * 4 + side * 2 + core


def remote(src, dst, send, recv, index):
    return pltpu.make_async_remote_copy(
        src_ref=src,
        dst_ref=dst,
        send_sem=send,
        recv_sem=recv,
        device_id={"dp": index},
        device_id_type=pl.DeviceIdType.MESH,
    )


def gather_kernel(layers, own_ref, full_ref, z_send, z_recv, y_send, y_recv, c_send, c_recv, local):
    me, depth, side, core = dp_place(layers * 4)
    deeper = [lax.rem(depth + step, layers) for step in range(1, layers)]
    y_peer = dp_index(depth, 1 - side, core)
    c_peer = dp_index(depth, side, 1 - core)
    greet([("dp", dp_index(d, side, core)) for d in deeper] + [("dp", y_peer), ("dp", c_peer)])
    sends = []

    def start(src, index, send, recv, target):
        copy = remote(src, full_ref.at[index], send, recv, target)
        copy.start()
        sends.append(copy)

    def arrived(index, recv):
        remote(full_ref.at[index], full_ref.at[index], local, recv, y_peer).wait_recv()

    keep = pltpu.make_async_copy(own_ref, full_ref.at[me], local)
    keep.start()
    start(own_ref, me, y_send.at[depth], y_recv.at[depth], y_peer)
    for d in deeper:
        start(own_ref, me, z_send.at[d], z_recv.at[depth], dp_index(d, side, core))
    start(own_ref, me, c_send.at[2 * depth + side], c_recv.at[2 * depth + side], c_peer)
    for d in deeper:
        index = dp_index(d, side, core)
        arrived(index, z_recv.at[d])
        start(full_ref.at[index], index, y_send.at[d], y_recv.at[d], y_peer)
        slot = 2 * d + side
        start(full_ref.at[index], index, c_send.at[slot], c_recv.at[slot], c_peer)
    for d in [depth] + deeper:
        index = dp_index(d, 1 - side, core)
        arrived(index, y_recv.at[d])
        slot = 2 * d + 1 - side
        start(full_ref.at[index], index, c_send.at[slot], c_recv.at[slot], c_peer)
    for d in [depth] + deeper:
        for s in (side, 1 - side):
            arrived(dp_index(d, s, 1 - core), c_recv.at[2 * d + s])
    keep.wait()
    for copy in sends:
        copy.wait_send()


def gather_dp(own):
    size = lax.axis_size("dp")
    layers = size // 4
    sem = pltpu.SemaphoreType.DMA
    full = pl.pallas_call(
        lambda *refs: gather_kernel(layers, *refs),
        out_shape=jax.ShapeDtypeStruct((size,) + own.shape, own.dtype),
        in_specs=[pl.BlockSpec(memory_space=pltpu.VMEM)],
        out_specs=pl.BlockSpec(memory_space=pltpu.VMEM),
        scratch_shapes=[
            sem((layers,)), sem((layers,)), sem((layers,)), sem((layers,)),
            sem((2 * layers,)), sem((2 * layers,)), sem,
        ],
        compiler_params=pltpu.CompilerParams(
            collective_id=1, has_side_effects=True, vmem_limit_bytes=40 * 1024 * 1024
        ),
        name="gather_dp",
    )(own)
    return full.reshape(size * own.shape[0], own.shape[1])


def reduce_kernel(
    layers, part_ref, out_ref, c_buf, y_out, y_buf, z_out, z_buf,
    c_send, c_recv, y_send, y_recv, z_send, z_recv,
):
    f32 = jnp.float32
    me, depth, side, core = dp_place(layers * 4)
    deeper = [lax.rem(depth + step, layers) for step in range(1, layers)]
    y_peer = dp_index(depth, 1 - side, core)
    c_peer = dp_index(depth, side, 1 - core)
    greet([("dp", dp_index(d, side, core)) for d in deeper] + [("dp", y_peer), ("dp", c_peer)])
    order = deeper + [depth]
    sends = []

    def start(src, dst, send, recv, target):
        copy = remote(src, dst, send, recv, target)
        copy.start()
        sends.append(copy)

    for s in (1 - side, side):
        for d in order:
            slot = 2 * d + s
            start(
                part_ref.at[dp_index(d, s, 1 - core)], c_buf.at[slot],
                c_send.at[slot], c_recv.at[slot], c_peer,
            )
    for d in order:
        slot = 2 * d + 1 - side
        remote(c_buf.at[slot], c_buf.at[slot], c_send.at[slot], c_recv.at[slot], c_peer).wait_recv()
        mine = part_ref[dp_index(d, 1 - side, core)].astype(f32)
        y_out[d] = (mine + c_buf[slot].astype(f32)).astype(y_out.dtype)
        start(y_out.at[d], y_buf.at[d], y_send.at[d], y_recv.at[d], y_peer)
    for d in order:
        slot = 2 * d + side
        remote(c_buf.at[slot], c_buf.at[slot], c_send.at[slot], c_recv.at[slot], c_peer).wait_recv()
        remote(y_buf.at[d], y_buf.at[d], y_send.at[d], y_recv.at[d], y_peer).wait_recv()
        total = part_ref[dp_index(d, side, core)].astype(f32) + c_buf[slot].astype(f32)
        total = total + y_buf[d].astype(f32)
        if d is not depth:
            z_out[d] = total.astype(z_out.dtype)
            start(
                z_out.at[d], z_buf.at[depth], z_send.at[d], z_recv.at[depth],
                dp_index(d, side, core),
            )
        else:
            out_ref[...] = total
    for d in deeper:
        remote(z_buf.at[d], z_buf.at[d], z_send.at[d], z_recv.at[d], y_peer).wait_recv()
        out_ref[...] += z_buf[d].astype(f32)
    for copy in sends:
        copy.wait_send()


def reduce_dp(part):
    size, rows, columns = part.shape
    layers = size // 4
    sem = pltpu.SemaphoreType.DMA
    block = lambda count: pltpu.VMEM((count, rows, columns), part.dtype)
    return pl.pallas_call(
        lambda *refs: reduce_kernel(layers, *refs),
        out_shape=jax.ShapeDtypeStruct((rows, columns), jnp.float32),
        in_specs=[pl.BlockSpec(memory_space=pltpu.VMEM)],
        out_specs=pl.BlockSpec(memory_space=pltpu.VMEM),
        scratch_shapes=[
            block(2 * layers), block(layers), block(layers), block(layers), block(layers),
            sem((2 * layers,)), sem((2 * layers,)), sem((layers,)), sem((layers,)),
            sem((layers,)), sem((layers,)),
        ],
        compiler_params=pltpu.CompilerParams(
            collective_id=2, has_side_effects=True, vmem_limit_bytes=60 * 1024 * 1024
        ),
        name="reduce_dp",
    )(part)


def swap(piece):
    return lax.ppermute(piece, "tensor", [(0, 1), (1, 0)])


def spread(piece):
    return jnp.concatenate([piece, swap(piece)], axis=0)


def mm(left, right, dims):
    return lax.dot_general(left, right, (dims, ((), ())), preferred_element_type=jnp.float32)


NN = ((1,), (0,))
NT = ((1,), (1,))
TN = ((0,), (0,))


def collect(lefts, rights, dims, own_rows):
    def term(first, last):
        total = None
        for left, right in zip(lefts, rights):
            now = mm(left[first:last], right, dims)
            total = now if total is None else total + now
        return total

    away = swap(term(own_rows, None).astype(jnp.bfloat16))
    return term(0, own_rows) + away.astype(jnp.float32)


def body(
    tokens,
    segment_ids,
    query_weight,
    key_weight,
    value_weight,
    out_weight,
    gate_weight,
    up_weight,
    down_weight,
    gain_before_attention,
    gain_after_attention,
    gain_before_feed,
    gain_after_feed,
    query_gain,
    key_gain,
    cotangent,
):
    f32 = jnp.float32
    bf16 = jnp.bfloat16
    own_rows = tokens.shape[0]
    total_rows = 2 * own_rows
    tensor_index = lax.axis_index("tensor")
    own_start = tensor_index * own_rows
    away_start = own_rows - own_start
    scale = HD ** (-0.5)
    shard_rows = key_weight.shape[0]
    head_rows = query_gain.shape[0]
    pad_head = lambda g: jnp.pad(g, (0, shard_rows - head_rows))
    gains = jnp.stack(
        [
            gain_before_attention, gain_after_attention, gain_before_feed, gain_after_feed,
            pad_head(query_gain), pad_head(key_gain),
        ],
        axis=1,
    )
    gains = jnp.pad(gains, ((0, 0), (0, 128 - gains.shape[1])))
    pieces = [query_weight, key_weight, value_weight, out_weight.T, gate_weight, up_weight, down_weight.T, gains]
    widths = [p.shape[1] for p in pieces]
    starts = [sum(widths[:i]) for i in range(len(widths) + 1)]
    full = gather_dp(jnp.concatenate(pieces, axis=1))
    query_full, key_full, value_full, out_t, gate_full, up_full, down_t, gain_full = [
        full[:, a:b] for a, b in zip(starts[:-1], starts[1:])
    ]
    gain_cols = gain_full[:, :8].astype(f32).T
    gain_ai, gain_ao, gain_fi, gain_fo = gain_cols[0], gain_cols[1], gain_cols[2], gain_cols[3]
    gain_query = gain_cols[4].reshape(-1, shard_rows)[:, :head_rows].reshape(-1)
    gain_key = gain_cols[5].reshape(-1, shard_rows)[:, :head_rows].reshape(-1)
    local_heads = query_full.shape[1] // HD
    offsets = jnp.arange(own_rows, dtype=jnp.int32)
    position = jnp.concatenate([own_start + offsets, away_start + offsets])
    segments = jnp.concatenate(
        [
            lax.dynamic_slice_in_dim(segment_ids, own_start, own_rows, 0),
            lax.dynamic_slice_in_dim(segment_ids, away_start, own_rows, 0),
        ]
    )
    x_rows = tokens.astype(f32)
    normed_in = spread(norm_fwd(x_rows, gain_ai).astype(bf16))
    queries = mm(normed_in, query_full, NN).reshape(total_rows, local_heads, HD)
    key_rows = mm(normed_in, key_full, NN)
    value_rows = mm(normed_in, value_full, NN).astype(bf16)
    cosine, sine_table = rope_tables(segments, position)
    query_rot = (
        rotate(norm_fwd(queries, gain_query), cosine[:, None, :], sine_table[:, None, :]) * scale
    ).astype(bf16)
    key_rot = rotate(norm_fwd(key_rows, gain_key), cosine, sine_table).astype(bf16)
    spacing = position[:, None] - position[None, :]
    allowed = (segments[:, None] == segments[None, :]) & (spacing >= 0) & (spacing < WINDOW)
    allowed = allowed[None]
    scores = jnp.einsum("qhd,kd->hqk", query_rot, key_rot, preferred_element_type=f32)
    exp_total = jnp.sum(jnp.where(allowed, jnp.exp(scores), 0.0), axis=-1, keepdims=True)
    log_total = jnp.log(exp_total)
    probs = jnp.where(allowed, jnp.exp(scores - log_total), 0.0)
    probs_b = probs.astype(bf16)
    attended = jnp.einsum("hqk,kd->qhd", probs_b, value_rows, preferred_element_type=f32)
    attended = attended.reshape(total_rows, local_heads * HD).astype(bf16)
    mixed = collect((attended,), (out_t,), NT, own_rows)
    hidden_state = x_rows + norm_fwd(mixed, gain_ao)
    normed_mid = spread(norm_fwd(hidden_state, gain_fi).astype(bf16))
    gate_pre = mm(normed_mid, gate_full, NN)
    up_values = mm(normed_mid, up_full, NN)
    gelu_value, gelu_slope = gelu_parts(gate_pre)
    activated = (gelu_value * up_values).astype(bf16)
    feed_out = collect((activated,), (down_t,), NT, own_rows)
    result = hidden_state + norm_fwd(feed_out, gain_fo)
    grad_feed, grad_gfo = norm_back(feed_out, gain_fo, cotangent)
    grad_feed_all = spread(grad_feed.astype(bf16))
    grad_act = mm(grad_feed_all, down_t, NN)
    grad_down_t = mm(grad_feed_all, activated, TN)
    grad_gate_b = (grad_act * up_values * gelu_slope).astype(bf16)
    grad_up_b = (grad_act * gelu_value).astype(bf16)
    grad_gate_w = mm(normed_mid, grad_gate_b, TN)
    grad_up_w = mm(normed_mid, grad_up_b, TN)
    grad_mid = collect((grad_gate_b, grad_up_b), (gate_full, up_full), NT, own_rows)
    grad_mid_in, grad_gfi = norm_back(hidden_state, gain_fi, grad_mid)
    grad_hidden = cotangent + grad_mid_in
    grad_mixed, grad_gao = norm_back(mixed, gain_ao, grad_hidden)
    grad_mixed_all = spread(grad_mixed.astype(bf16))
    grad_attended = mm(grad_mixed_all, out_t, NN).astype(bf16)
    grad_out_t = mm(grad_mixed_all, attended, TN)
    grad_heads = grad_attended.reshape(total_rows, local_heads, HD)
    grad_probs = jnp.einsum("qhd,kd->hqk", grad_heads, value_rows, preferred_element_type=f32)
    grad_scores = (
        probs * (grad_probs - jnp.sum(probs * grad_probs, axis=-1, keepdims=True))
    ).astype(bf16)
    grad_qrot = jnp.einsum("hqk,kd->qhd", grad_scores, key_rot, preferred_element_type=f32)
    grad_krot = jnp.einsum("hqk,qhd->kd", grad_scores, query_rot, preferred_element_type=f32)
    grad_vpart = jnp.einsum("hqk,qhd->kd", probs_b, grad_heads, preferred_element_type=f32)
    pair = jnp.concatenate([grad_krot, grad_vpart], axis=1)
    pair_away = swap(pair[own_rows:].astype(bf16)).astype(f32)
    pair_own = pair[:own_rows] + pair_away
    grad_kunit = unrotate(pair_own[:, :HD], cosine[:own_rows], sine_table[:own_rows])
    grad_value_b = pair_own[:, HD:].astype(bf16)
    grad_qunit = unrotate(grad_qrot * scale, cosine[:, None, :], sine_table[:, None, :])
    grad_queries, grad_gq = norm_back(queries, gain_query, grad_qunit)
    grad_keys, grad_gk = norm_back(key_rows[:own_rows], gain_key, grad_kunit)
    grad_queries_b = grad_queries.reshape(total_rows, local_heads * HD).astype(bf16)
    grad_keys_b = grad_keys.astype(bf16)
    normed_own = normed_in[:own_rows]
    grad_query_w = mm(normed_in, grad_queries_b, TN)
    grad_key_w = mm(normed_own, grad_keys_b, TN)
    grad_value_w = mm(normed_own, grad_value_b, TN)
    grad_normed = (
        collect((grad_queries_b,), (query_full,), NT, own_rows)
        + mm(grad_keys_b, key_full, NT)
        + mm(grad_value_b, value_full, NT)
    )
    grad_in_rows, grad_gai = norm_back(x_rows, gain_ai, grad_normed)
    grad_tokens = grad_hidden + grad_in_rows
    pad_gain = lambda g: jnp.pad(
        g.reshape(-1, head_rows), ((0, 0), (0, shard_rows - head_rows))
    ).reshape(-1)
    gain_grads = jnp.stack(
        [grad_gai, grad_gao, grad_gfi, grad_gfo, pad_gain(grad_gq), pad_gain(grad_gk)], axis=1
    )
    gain_grads = jnp.pad(gain_grads, ((0, 0), (0, 128 - gain_grads.shape[1])))
    parts = [
        grad_query_w, grad_key_w, grad_value_w, grad_out_t, grad_gate_w, grad_up_w, grad_down_t,
        gain_grads,
    ]
    packed = jnp.concatenate([p.astype(bf16) for p in parts], axis=1)
    total = reduce_dp(packed.reshape(-1, shard_rows, packed.shape[1]))
    shards = [total[:, a:b] for a, b in zip(starts[:-1], starts[1:])]
    shared = jnp.concatenate([shards[1], shards[2], shards[7]], axis=1)
    shared = shared + swap(shared)
    key_shard = shared[:, :HD]
    value_shard = shared[:, HD : 2 * HD]
    gain_shard = shared[:, 2 * HD :]
    return (
        result,
        grad_tokens,
        shards[0],
        key_shard,
        value_shard,
        shards[3].T,
        shards[4],
        shards[5],
        shards[6].T,
        gain_shard[:, 0],
        gain_shard[:, 1],
        gain_shard[:, 2],
        gain_shard[:, 3],
        gain_shard[:head_rows, 4],
        gain_shard[:head_rows, 5],
    )


def solution(mesh):
    in_specs = (
        P(("dp", "tensor"), None),
        P("dp"),
        P("dp", "tensor"),
        P("dp", None),
        P("dp", None),
        P("tensor", "dp"),
        P("dp", "tensor"),
        P("dp", "tensor"),
        P("tensor", "dp"),
        P("dp"),
        P("dp"),
        P("dp"),
        P("dp"),
        P("dp"),
        P("dp"),
        P(("dp", "tensor"), None),
    )
    out_specs = (
        P(("dp", "tensor"), None),
        P(("dp", "tensor"), None),
        P("dp", "tensor"),
        P("dp", None),
        P("dp", None),
        P("tensor", "dp"),
        P("dp", "tensor"),
        P("dp", "tensor"),
        P("tensor", "dp"),
        P("dp"),
        P("dp"),
        P("dp"),
        P("dp"),
        P("dp"),
        P("dp"),
    )
    return jax.shard_map(body, mesh=mesh, in_specs=in_specs, out_specs=out_specs, check_vma=False)
```

time: 875 us -> 284 us (0.32)
  waiting for transfers between devices: 525 us -> 40.7 us
  blocking collectives: 221 us -> 0 us
  Pallas kernels: 0 us -> 116 us
  between operations: 19.5 us -> 1.63 us
  local copies, waits for them, and re-layouts: 20.8 us -> 37.7 us
  other arithmetic: 32.2 us -> 16.8 us
  starting transfers between devices: 0.84 us -> 14.4 us
    reduce_scatter x11 -> x0, waiting for transfers between devices: 425 us -> none  [the longest x1 67.6 us: body(): lax.psum_scatter(grad_up_w, 'dp', scatter_dimension=0, tiled=True)]
    all_gather x8 -> x0, blocking collectives: 118 us -> none  [the longest x1 22.3 us: body(): lax.all_gather(out_weight, 'dp', axis=1, tiled=True)]
    pallas_call x0 -> x2, Pallas kernels: none -> 116 us  [the longest x1 63.9 us: reduce_dp(): pl.pallas_call(lambda *refs: reduce_kernel(layers, *refs), out_shape=jax....]
    unnamed x2 -> x0, blocking collectives: 97.6 us -> none
    all_gather x3 -> x0, waiting for transfers between devices: 76.4 us -> none  [the longest x1 36.3 us: body(): lax.all_gather(up_weight, 'dp', axis=0, tiled=True)]
    ppermute x0 -> x10, waiting for transfers between devices: none -> 40.7 us  [swap(): return lax.ppermute(piece, 'tensor', [(0, 1), (1, 0)])]
    psum x1 -> x0, waiting for transfers between devices: 22.1 us -> none  [body(): lax.psum(grad_krot.astype(jnp.bfloat16), 'tensor').astype(jnp.float32)]
    ppermute x0 -> x10, starting transfers between devices: none -> 14.4 us  [swap(): return lax.ppermute(piece, 'tensor', [(0, 1), (1, 0)])]
  transfers between devices with their start and end apart: 15 -> 10, of which waited for: 13 -> 8; matrix products, arithmetic and copies ran while one was open for 5% -> 12% of each run, Pallas kernels for 0% -> 0%
where the time goes in v1:
time: 284 us; the launch traced here: 282 us
  Pallas kernels  116 us (41%)
  matrix products  55.4 us (20%)
  waiting for transfers between devices  40.7 us (14%)
  local copies, waits for them, and re-layouts  37.7 us (13%)
  other arithmetic  16.8 us (6%)
  starting transfers between devices  14.4 us (5%)
    pallas_call x1, Pallas kernels, reduce_dp(): pl.pallas_call(lambda *refs: reduce_kernel(layers, *refs), out_shape=jax....  63.9 us
    pallas_call x1, Pallas kernels, gather_dp(): pl.pallas_call(lambda *refs: gather_kernel(layers, *refs), out_shape=jax....  51.9 us
    dot_general x26, matrix products, mm(): lax.dot_general(left, right, (dims, ((), ())), preferred_element_type=jnp...  44.3 us
    ppermute x10, waiting for transfers between devices, swap(): return lax.ppermute(piece, 'tensor', [(0, 1), (1, 0)])  40.7 us
    unnamed x148, local copies, waits for them, and re-layouts  15.1 us
    ppermute x10, starting transfers between devices, swap(): return lax.ppermute(piece, 'tensor', [(0, 1), (1, 0)])  14.4 us
  transfers between devices with their start and end apart: 10, of which 8 were waited for; matrix products, arithmetic and copies ran while one was open for 12% of the time, Pallas kernels for 0%

profile of v1, /device:TPU:0, one launch (start us, length us, event | category | flops | bytes accessed | tf_op | source)
XLA Modules:
  0.0 282.4 jit_solution(10992954026843826316)
XLA Ops:
  9.0 51.9 %gather_dp.1 = bf16[16,40,4736]{2,1,0:T(8,128)(2,1)S(1)} custom-call(bf16[40,4736]{1,0:T(8,128)(2,1)S(1)} %constant_dynamic-update-slice_fusion.refs_0_), custom_call_target="tpu_custom_call" | custom-call | tf_op jit(solution)/shard_map/gather_dp/pallas_call | solution.py:148
  60.9 2.6 copy-done
  67.2 6.8 %collective-permute-done = bf16[256,640]{1,0:T(8,128)(2,1)S(1)} collective-permute-done((bf16[256,640]{1,0:T(8,128)(2,1)S(1)}, bf16[256,640]{1,0:T(8,128)(2,1)S(1)}, u32[]{:S(2)}, u32[]{:S(2)}) %collective-permute-start) | collective-permute-done | bytes 327712 | tf_op jit(solution)/shard_map/ppermute | solution.py:240
  76.4 1.8 multiply_cosine_fusion
  80.0 1.7 multiply_reduce_fusion.1
  83.7 1.8 fusion.108
  85.5 2.0 fusion.23
  87.6 4.5 %convolution_convert_fusion.6 = bf16[256,2,512]{2,0,1:T(8,128)(2,1)} fusion(bf16[512,256,1]{1,0,2:T(8,128)(2,1)} %fusion.23, f32[512,512,2]{1,0,2:T(8,128)} %fusion.108, pred[512,512]{0,1:T(8,128)(4,1)} %fusion.31), kind=kOutput, calls=%fused_computation.39 | convolution fusion | flops 270796288 | bytes 3145728 | tf_op jit(solution)/shard_map/hqk,kd->qhd/dot_general | solution.py:343
  96.2 7.7 %collective-permute-done.1 = bf16[256,640]{1,0:T(8,128)(2,1)S(1)} collective-permute-done((bf16[256,640]{1,0:T(8,128)(2,1)S(1)}, bf16[256,640]{1,0:T(8,128)(2,1)S(1)}, u32[]{:S(2)}, u32[]{:S(2)}) %collective-permute-start.1) | collective-permute-done | bytes 327712 | tf_op jit(solution)/shard_map/ppermute | solution.py:240
  103.8 1.7 multiply_reduce_fusion.10
  107.6 6.8 %collective-permute-done.2 = bf16[256,640]{1,0:T(8,128)(2,1)S(1)} collective-permute-done((bf16[256,640]{1,0:T(8,128)(2,1)S(1)}, bf16[256,640]{1,0:T(8,128)(2,1)S(1)}, u32[]{:S(2)}, u32[]{:S(2)}) %collective-permute-start.2) | collective-permute-done | bytes 327712 | tf_op jit(solution)/shard_map/ppermute | solution.py:240
  114.4 2.4 fusion.46
  120.3 6.0 %collective-permute-done.3 = bf16[256,640]{1,0:T(8,128)(2,1)S(1)} collective-permute-done((bf16[256,640]{1,0:T(8,128)(2,1)S(1)}, bf16[256,640]{1,0:T(8,128)(2,1)S(1)}, u32[]{:S(2)}, u32[]{:S(2)}) %collective-permute-start.3) | collective-permute-done | bytes 327712 | tf_op jit(solution)/shard_map/ppermute | solution.py:240
  129.9 5.6 %collective-permute-done.4 = bf16[256,640]{1,0:T(8,128)(2,1)S(1)} collective-permute-done((bf16[256,640]{1,0:T(8,128)(2,1)S(1)}, bf16[256,640]{1,0:T(8,128)(2,1)S(1)}, u32[]{:S(2)}, u32[]{:S(2)}) %collective-permute-start.4) | collective-permute-done | bytes 327712 | tf_op jit(solution)/shard_map/ppermute | solution.py:240
  135.5 2.5 multiply_convert_fusion
  141.7 1.6 copy.109
  144.5 2.2 fusion.44
  147.3 2.1 multiply_reduce_fusion.3
  151.8 5.5 %collective-permute-done.6 = bf16[256,640]{1,0:T(8,128)(2,1)S(1)} collective-permute-done((bf16[256,640]{1,0:T(8,128)(2,1)S(1)}, bf16[256,640]{1,0:T(8,128)(2,1)S(1)}, u32[]{:S(2)}, u32[]{:S(2)}) %collective-permute-start.6) | collective-permute-done | bytes 327712 | tf_op jit(solution)/shard_map/ppermute | solution.py:240
  157.3 2.6 convolution_convert_fusion.5
  160.0 2.3 convolution_bitcast_fusion
  173.1 2.3 copy.115
  182.0 2.4 convolution_convert_fusion.9
  188.8 2.4 fusion.85
  196.3 3.1 %fusion.20 = bf16[640,4736]{1,0:T(8,128)(2,1)} fusion(bf16[640,4736]{1,0:T(8,128)(2,1)} %constant_dynamic-update-slice_fusion.6, bf16[512,1024]{1,0:T(8,128)(2,1)S(1)} %copy-done.63, bf16[256,640]{1,0:T(8,128)(2,1)} %copy-done.53, bf16[256,640]{1,0:T(8,128)(2,1)S(1)} %copy-done.44), kind=kOutput, calls=%fused_computation.29 | convolution fusion | flops 673054720 | bytes 3014656 | tf_op jit(solution)/shard_map/dot_general | solution.py:248
  199.4 2.0 fusion.19
  202.9 3.3 %fusion.18 = bf16[640,4736]{1,0:T(8,128)(2,1)} fusion(bf16[640,4736]{1,0:T(8,128)(2,1)} %fusion.19, bf16[512,1024]{1,0:T(8,128)(2,1)} %copy-done.64, bf16[256,640]{1,0:T(8,128)(2,1)S(1)} %copy-done.56, bf16[256,640]{1,0:T(8,128)(2,1)S(1)} %copy-done.42), kind=kOutput, calls=%fused_computation.25 | convolution fusion | flops 673054720 | bytes 3014656 | tf_op jit(solution)/shard_map/dot_general | solution.py:248
  206.2 1.6 fusion.57
  208.7 63.9 %reduce_dp.1 = f32[40,4736]{1,0:T(8,128)} custom-call(bf16[16,40,4736]{2,1,0:T(8,128)(2,1)} %bitcast.143), custom_call_target="tpu_custom_call" | custom-call | tf_op jit(solution)/shard_map/reduce_dp/pallas_call | solution.py:222
  273.4 1.6 slice_bitcast_fusion.1
  275.1 1.6 collective-permute-start.9
  278.6 1.7 collective-permute-done.9
  (263 shorter events, 72.6 us)
Async XLA Ops:
  9.0 54.7 %copy-start.6 = (bf16[256,640]{1,0:T(8,128)(2,1)S(1)}, bf16[256,640]{1,0:T(8,128)(2,1)}, u32[]{:S(2)}) copy-start(bf16[256,640]{1,0:T(8,128)(2,1)} %param.16) | copy-start | bytes 983044
  9.0 56.4 %copy-start.49 = (s32[512]{0:T(512)S(1)}, s32[512]{0:T(512)}, u32[]{:S(2)}) copy-start(s32[512]{0:T(512)} %param.17) | copy-start | bytes 6148
  63.9 16.1 %copy-start.21 = (bf16[256,640]{1,0:T(8,128)(2,1)}, bf16[256,640]{1,0:T(8,128)(2,1)S(1)}, u32[]{:S(2)}) copy-start(bf16[256,640]{1,0:T(8,128)(2,1)S(1)} %fusion.52) | copy-start | bytes 983044
  63.9 10.1 %collective-permute-start = (bf16[256,640]{1,0:T(8,128)(2,1)S(1)}, bf16[256,640]{1,0:T(8,128)(2,1)S(1)}, u32[]{:S(2)}, u32[]{:S(2)}) collective-permute-start(bf16[256,640]{1,0:T(8,128)(2,1)S(1)} %fusion.52), channel_id=1, source_target_pairs={{0,1},{1,0},{2,3},{3,2},{4,5},{5,4},{6,7},{7,6},{8,9},{9,8},{10,11... | collective-permute-start | bytes 983048 | tf_op jit(solution)/shard_map/ppermute | solution.py:240
  73.9 6.0 %copy-start.50 = (bf16[256,640]{1,0:T(8,128)(2,1)}, bf16[256,640]{1,0:T(8,128)(2,1)S(1)}, u32[]{:S(2)}) copy-start(bf16[256,640]{1,0:T(8,128)(2,1)S(1)} %collective-permute-done) | copy-start | bytes 983044
  83.6 3.9 %copy-start.11 = (f32[512,2,128]{2,0,1:T(8,128)}, f32[512,2,128]{2,0,1:T(8,128)S(1)}, u32[]{:S(2)}) copy-start(f32[512,2,128]{2,0,1:T(8,128)S(1)} %get-tuple-element.44) | copy-start | bytes 1572868
  87.6 29.3 %slice-start = ((s8[6062080]{0:T(1024)(128)(4,1)}), s8[1867776]{0:T(1024)(128)(4,1)S(1)}, s32[]{:S(2)}) async-start(s8[6062080]{0:T(1024)(128)(4,1)} %bitcast.134), calls=%async_computation | async-start | bytes 3735552
  94.6 9.2 %collective-permute-start.1 = (bf16[256,640]{1,0:T(8,128)(2,1)S(1)}, bf16[256,640]{1,0:T(8,128)(2,1)S(1)}, u32[]{:S(2)}, u32[]{:S(2)}) collective-permute-start(bf16[256,640]{1,0:T(8,128)(2,1)S(1)} %convolution_convert_fusion.11), channel_id=1, source_target_pairs={{0,1},{1,0},{2,3},{3,2},{4,5},{5,4},{6,7},{7,6},{8,9},{9,8},{10,11... | collective-permute-start | bytes 983048 | tf_op jit(solution)/shard_map/ppermute | solution.py:240
  103.8 13.1 %slice-start.1 = ((s8[6062080]{0:T(1024)(128)(4,1)}), s8[4194304]{0:T(1024)(128)(4,1)S(1)}, s32[]{:S(2)}) async-start(s8[6062080]{0:T(1024)(128)(4,1)} %bitcast.134), calls=%async_computation.1 | async-start | bytes 8388608
  106.0 10.8 %copy-start.43 = (bf16[256,640]{1,0:T(8,128)(2,1)}, bf16[256,640]{1,0:T(8,128)(2,1)S(1)}, u32[]{:S(2)}) copy-start(bf16[256,640]{1,0:T(8,128)(2,1)S(1)} %multiply_convert_fusion.4) | copy-start | bytes 983044
  106.0 8.4 %collective-permute-start.2 = (bf16[256,640]{1,0:T(8,128)(2,1)S(1)}, bf16[256,640]{1,0:T(8,128)(2,1)S(1)}, u32[]{:S(2)}, u32[]{:S(2)}) collective-permute-start(bf16[256,640]{1,0:T(8,128)(2,1)S(1)} %multiply_convert_fusion.4), channel_id=1, source_target_pairs={{0,1},{1,0},{2,3},{3,2},{4,5},{5,4},{6,7},{7,6},{8,9},{9,8},{10,11... | collective-permute-start | bytes 983048 | tf_op jit(solution)/shard_map/ppermute | solution.py:240
  118.2 8.9 %copy-start.64 = (bf16[512,1024]{1,0:T(8,128)(2,1)}, bf16[512,1024]{1,0:T(8,128)(2,1)S(1)}, u32[]{:S(2)}) copy-start(bf16[512,1024]{1,0:T(8,128)(2,1)S(1)} %get-tuple-element.78) | copy-start | bytes 3145732
  118.8 8.3 %copy-start.7 = (f32[256,640]{1,0:T(8,128)S(1)}, f32[256,640]{1,0:T(8,128)}, u32[]{:S(2)}) copy-start(f32[256,640]{1,0:T(8,128)} %param.31) | copy-start | bytes 1966084
  118.8 7.5 %collective-permute-start.3 = (bf16[256,640]{1,0:T(8,128)(2,1)S(1)}, bf16[256,640]{1,0:T(8,128)(2,1)S(1)}, u32[]{:S(2)}, u32[]{:S(2)}) collective-permute-start(bf16[256,640]{1,0:T(8,128)(2,1)S(1)} %convolution_convert_fusion.10), channel_id=1, source_target_pairs={{0,1},{1,0},{2,3},{3,2},{4,5},{5,4},{6,7},{7,6},{8,9},{9,8},{10,11... | collective-permute-start | bytes 983048 | tf_op jit(solution)/shard_map/ppermute | solution.py:240
  128.4 9.6 %copy-start.41 = (bf16[256,640]{1,0:T(8,128)(2,1)}, bf16[256,640]{1,0:T(8,128)(2,1)S(1)}, u32[]{:S(2)}) copy-start(bf16[256,640]{1,0:T(8,128)(2,1)S(1)} %get-tuple-element.56) | copy-start | bytes 983044
  128.4 7.1 %collective-permute-start.4 = (bf16[256,640]{1,0:T(8,128)(2,1)S(1)}, bf16[256,640]{1,0:T(8,128)(2,1)S(1)}, u32[]{:S(2)}, u32[]{:S(2)}) collective-permute-start(bf16[256,640]{1,0:T(8,128)(2,1)S(1)} %get-tuple-element.56), channel_id=1, source_target_pairs={{0,1},{1,0},{2,3},{3,2},{4,5},{5,4},{6,7},{7,6},{8,9},{9,8},{10,11... | collective-permute-start | bytes 983048 | tf_op jit(solution)/shard_map/ppermute | solution.py:240
  140.0 7.3 %collective-permute-start.5 = (bf16[256,640]{1,0:T(8,128)(2,1)}, bf16[256,640]{1,0:T(8,128)(2,1)S(1)}, u32[]{:S(2)}, u32[]{:S(2)}) collective-permute-start(bf16[256,640]{1,0:T(8,128)(2,1)} %fusion.22), channel_id=1, source_target_pairs={{0,1},{1,0},{2,3},{3,2},{4,5},{5,4},{6,7},{7,6},{8,9},{9,8},{10,11... | collective-permute-start | bytes 983048 | tf_op jit(solution)/shard_map/ppermute | solution.py:240
  149.9 10.0 %copy-start.9 = (f32[256,640]{1,0:T(8,128)}, f32[256,640]{1,0:T(8,128)S(1)}, u32[]{:S(2)}) copy-start(f32[256,640]{1,0:T(8,128)S(1)} %get-tuple-element.37) | copy-start | bytes 1966084
  150.1 9.8 %copy-start.46 = (bf16[256,640]{1,0:T(8,128)(2,1)}, bf16[256,640]{1,0:T(8,128)(2,1)S(1)}, u32[]{:S(2)}) copy-start(bf16[256,640]{1,0:T(8,128)(2,1)S(1)} %multiply_convert_fusion.2) | copy-start | bytes 983044
  150.1 9.8 %copy-start.5 = (f32[512,512,2]{1,0,2:T(8,128)S(1)}, f32[512,512,2]{1,0,2:T(8,128)}, u32[]{:S(2)}) copy-start(f32[512,512,2]{1,0,2:T(8,128)} %fusion.108) | copy-start | bytes 6291460
  150.1 9.8 %copy-start.39 = (pred[512,512]{0,1:T(8,128)(4,1)S(1)}, pred[512,512]{0,1:T(8,128)(4,1)}, u32[]{:S(2)}) copy-start(pred[512,512]{0,1:T(8,128)(4,1)} %fusion.31) | copy-start | bytes 786436
  150.1 7.1 %collective-permute-start.6 = (bf16[256,640]{1,0:T(8,128)(2,1)S(1)}, bf16[256,640]{1,0:T(8,128)(2,1)S(1)}, u32[]{:S(2)}, u32[]{:S(2)}) collective-permute-start(bf16[256,640]{1,0:T(8,128)(2,1)S(1)} %multiply_convert_fusion.2), channel_id=1, source_target_pairs={{0,1},{1,0},{2,3},{3,2},{4,5},{5,4},{6,7},{7,6},{8,9},{9,8},{10,11... | collective-permute-start | bytes 983048 | tf_op jit(solution)/shard_map/ppermute | solution.py:240
  173.1 6.1 %copy-start.16 = (f32[512,2,256]{2,0,1:T(8,128)S(1)}, f32[512,2,256]{2,0,1:T(8,128)}, u32[]{:S(2)}) copy-start(f32[512,2,256]{2,0,1:T(8,128)} %get-tuple-element.47) | copy-start | bytes 3145732
  177.7 13.6 %collective-permute-start.8 = (bf16[256,512]{0,1:T(8,128)(2,1)}, bf16[256,512]{0,1:T(8,128)(2,1)}, u32[]{:S(2)}, u32[]{:S(2)}) collective-permute-start(bf16[256,512]{0,1:T(8,128)(2,1)} %fusion.61), channel_id=1, source_target_pairs={{0,1},{1,0},{2,3},{3,2},{4,5},{5,4},{6,7},{7,6},{8,9},{9,8},{10,11... | collective-permute-start | bytes 786440 | tf_op jit(solution)/shard_map/ppermute | solution.py:240
  180.5 4.0 %copy-start.23 = (bf16[256,640]{1,0:T(8,128)(2,1)S(1)}, bf16[256,640]{1,0:T(8,128)(2,1)}, u32[]{:S(2)}) copy-start(bf16[256,640]{1,0:T(8,128)(2,1)} %copy-done.21) | copy-start | bytes 983044
  180.5 4.0 %copy-start.52 = (bf16[256,640]{1,0:T(8,128)(2,1)S(1)}, bf16[256,640]{1,0:T(8,128)(2,1)}, u32[]{:S(2)}) copy-start(bf16[256,640]{1,0:T(8,128)(2,1)} %copy-done.50) | copy-start | bytes 983044
  187.3 5.1 %copy-start.31 = (f32[512,128]{0,1:T(8,128)S(1)}, f32[512,128]{0,1:T(8,128)}, u32[]{:S(2)}) copy-start(f32[512,128]{0,1:T(8,128)} %copy-done.30) | copy-start | bytes 786436
  187.3 5.1 %copy-start.33 = (f32[512,128]{0,1:T(8,128)S(1)}, f32[512,128]{0,1:T(8,128)}, u32[]{:S(2)}) copy-start(f32[512,128]{0,1:T(8,128)} %copy-done.32) | copy-start | bytes 786436
  187.3 18.9 %collective-permute-start.7 = (bf16[256,640]{1,0:T(8,128)(2,1)}, bf16[256,640]{1,0:T(8,128)(2,1)}, u32[]{:S(2)}, u32[]{:S(2)}) collective-permute-start(bf16[256,640]{1,0:T(8,128)(2,1)} %convolution_convert_fusion.9), channel_id=1, source_target_pairs={{0,1},{1,0},{2,3},{3,2},{4,5},{5,4},{6,7},{7,6},{8,9},{9,8},{10,11... | collective-permute-start | bytes 983048 | tf_op jit(solution)/shard_map/ppermute | solution.py:240
  208.7 68.0 %copy-start.10 = (f32[256,640]{1,0:T(8,128)S(1)}, f32[256,640]{1,0:T(8,128)}, u32[]{:S(2)}) copy-start(f32[256,640]{1,0:T(8,128)} %copy-done.9) | copy-start | bytes 1966084
  272.6 5.2 %copy-start.20 = (f32[40,4736]{1,0:T(8,128)S(1)}, f32[40,4736]{1,0:T(8,128)}, u32[]{:S(2)}) copy-start(f32[40,4736]{1,0:T(8,128)} %reduce_dp.1) | copy-start | bytes 2273284
  275.1 5.2 %collective-permute-start.9 = (f32[40,640]{1,0:T(8,128)S(1)}, f32[40,640]{1,0:T(8,128)S(1)}, u32[]{:S(2)}, u32[]{:S(2)}) collective-permute-start(f32[40,640]{1,0:T(8,128)S(1)} %pad_maximum_fusion.11), channel_id=1, source_target_pairs={{0,1},{1,0},{2,3},{3,2},{4,5},{5,4},{6,7},{7,6},{8,9},{9,8},{10,11... | collective-permute-start | bytes 307208 | tf_op jit(solution)/shard_map/ppermute | solution.py:240
  (45 other events, 101.4 us)
